TPU v7x, 32 devices: a whole 2x2x4 slice. The times are simulated.
32 devices in a mesh: section: 4 (over z), dp: 4 (over x, core), tensor: 2 (over y).
Axes of the slice: x: 2, y: 2, z: 4, core: 2. Of those that a mesh axis runs over, the one named last changes fastest.
Arguments:
- activations: bfloat16 [4, 512, 4096], P('section', 'dp', 'tensor'), may hold values from -32 to 32
- norm_gain: float32 [4, 4096], P('section', 'tensor'), may hold values from 0.5 to 2
- weights: bfloat16 [4, 4096, 1024], P('section', 'tensor'), may hold values from -0.09375 to 0.09375
- cotangent: bfloat16 [4, 512, 1024], P('section', 'dp'), may hold values from -16 to 16
- top_grad: bfloat16 [512, 4096], P('dp', 'tensor'), may hold values from -6 to 6
- owner_slot: int32 [4, 2, 13], P('section', 'tensor'), may hold values from 0 to 15, as said below
- sweeps: int32 [4, 2, 4], P('section', 'tensor'), may hold values from 3 to 6
Outputs:
- input_grad: bfloat16 [4, 512, 4096], P('section', 'dp', 'tensor')
- preconditioned: bfloat16 [4, 4096, 1024], P('section', 'tensor')
Inputs may be any that keep to these rules, and one draw needn't show every extreme that they name: For each section and tensor index the 13 entries are distinct; the unit is owned by data replica owner_slot // 4, so a replica owns at most 4 units, and some replica owns exactly 4.
All inputs are finite; a program needn't handle non-finite values.
Results may differ from a plain program's by a relative error of at most 0.035.
Values may be sent and summed in bfloat16 or wider, within the bound.
No kernel may reach another device: no remote copies, remote signals or barrier semaphores. Data moves between devices by JAX's collectives and lax.ppermute only.
A program may use at most 128 MiB of HBM per device.

v0:
```python
import jax
import jax.numpy as jnp
from jax import lax
from jax.sharding import PartitionSpec as P

BLOCK = 512
ITERS = 6
EPSILON = 1e-05
DAMPING = 0.05
HIGHEST_PREC = lax.Precision.HIGHEST


def entering(value, axis, combine, identity):
    count, index = (lax.axis_size(axis), lax.axis_index(axis))
    everything = lax.all_gather(value.astype(jnp.bfloat16), axis)
    start = jnp.broadcast_to(jnp.asarray(identity, value.dtype), value.shape)

    def turn(k, before):
        at = count - 1 - k
        reached = at > index
        new = combine(before, everything[at].astype(value.dtype))
        return jnp.where(reached, new, before)

    return lax.fori_loop(0, count, turn, start)


def add_arrays(first_part, second_part):
    return first_part + second_part


def newton_schulz(matrices, limits):
    order_size = matrices.shape[-1]
    identity = jnp.eye(order_size, dtype=jnp.float32)
    frobenius = jnp.sqrt(jnp.sum(matrices * matrices, axis=(1, 2)))
    approx = identity[None] / frobenius[:, None, None]
    for each_sweep in range(ITERS):
        product = jnp.einsum("cij,cjk->cik", matrices, approx, precision=HIGHEST_PREC)
        update = jnp.einsum(
            "cij,cjk->cik", approx, 2.0 * identity[None] - product, precision=HIGHEST_PREC
        )
        approx = jnp.where((each_sweep < limits)[:, None, None], update, approx)
    return approx


def on_device(activations, norm_gain, weights, cotangent, top_grad, owner_slot, sweeps):
    inputs = activations[0].astype(jnp.float32)
    gain_row = norm_gain[0]
    weight_half = weights[0]
    upstream_v = cotangent[0]
    slot_table = owner_slot[0, 0]
    replica_limits = sweeps[0, 0]
    token_count, half_width = inputs.shape
    value_width = weight_half.shape[1]
    tensor_size = lax.axis_size("tensor")
    replica_count = lax.axis_size("dp")
    full_width = half_width * tensor_size
    feature_blocks = half_width // BLOCK
    value_blocks = value_width // BLOCK
    unit_count = feature_blocks + 1 + feature_blocks * value_blocks
    capacity = (unit_count + replica_count - 1) // replica_count
    slot_count = capacity * replica_count
    upstream = lax.dot_general(
        upstream_v, weight_half, (((1,), (1,)), ((), ())), preferred_element_type=jnp.float32
    )
    scaled = upstream * gain_row[None]
    own_squares = jnp.sum(inputs * inputs, axis=1)
    own_inner = jnp.sum(scaled * inputs, axis=1)
    squares, inner_sum = lax.psum((own_squares, own_inner), "tensor")
    inverse_rms = lax.rsqrt(squares / full_width + EPSILON)
    normed = (inputs * inverse_rms[:, None] * gain_row[None]).astype(jnp.bfloat16)
    own_term = (
        inverse_rms[:, None] * scaled
        - inputs * (inverse_rms * inverse_rms * inverse_rms * inner_sum / full_width)[:, None]
    )
    later_sum = entering(own_term, "section", add_arrays, jnp.zeros_like(own_term))
    input_grad = (top_grad.astype(jnp.float32) + later_sum + own_term).astype(jnp.bfloat16)[None]
    normed_blocks = normed.reshape(token_count, feature_blocks, BLOCK)
    value_parts = upstream_v.reshape(token_count, value_blocks, BLOCK)
    feature_units = jnp.einsum(
        "tia,tib->iab", normed_blocks, normed_blocks, preferred_element_type=jnp.float32
    )
    tensor_rank = lax.axis_index("tensor")
    own_values = lax.dynamic_slice_in_dim(upstream_v, tensor_rank * BLOCK, BLOCK, 1)
    value_unit = lax.dot_general(
        own_values, own_values, (((0,), (0,)), ((), ())), preferred_element_type=jnp.float32
    )
    grad_units = jnp.einsum(
        "tia,tjb->ijab", normed_blocks, value_parts, preferred_element_type=jnp.float32
    )
    grad_units = grad_units.reshape(feature_blocks * value_blocks, BLOCK, BLOCK)
    all_units = jnp.concatenate([feature_units, value_unit[None], grad_units], axis=0)
    slot_ids = jnp.arange(slot_count, dtype=jnp.int32)
    unit_ids = jnp.arange(unit_count, dtype=jnp.int32)
    matches = slot_table[None, :] == slot_ids[:, None]
    slot_unit = jnp.sum(jnp.where(matches, unit_ids[None, :] + 1, 0), axis=1) - 1
    filled = slot_unit >= 0
    packed = jnp.where(
        filled[:, None, None], jnp.take(all_units, jnp.maximum(slot_unit, 0), axis=0), 0.0
    )
    summed = lax.psum_scatter(
        packed.astype(jnp.bfloat16), "dp", scatter_dimension=0, tiled=True
    ).astype(jnp.float32)
    replica_rank = lax.axis_index("dp")
    first_slot = replica_rank * capacity
    own_units = lax.dynamic_slice_in_dim(slot_unit, first_slot, capacity, 0)
    is_factor = (own_units >= 0) & (own_units <= feature_blocks)
    identity = jnp.eye(BLOCK, dtype=jnp.float32)
    matrices = jnp.where(
        is_factor[:, None, None],
        summed / (token_count * replica_count) + DAMPING * identity[None],
        identity[None],
    )
    own_limit = lax.dynamic_slice_in_dim(replica_limits, replica_rank, 1, 0)
    own_limits = jnp.broadcast_to(own_limit, (capacity,))
    inverses = newton_schulz(matrices, own_limits)
    owned_blocks = jnp.where(is_factor[:, None, None], inverses, summed).astype(jnp.bfloat16)
    gathered = lax.all_gather(owned_blocks, "dp", axis=0, tiled=True)
    value_inverse = jnp.take(gathered, slot_table[feature_blocks], axis=0)
    value_inverses = lax.all_gather(value_inverse[None], "tensor", axis=0, tiled=True)
    feature_all = jnp.take(gathered, slot_table[:feature_blocks], axis=0)
    grad_all = jnp.take(gathered, slot_table[feature_blocks + 1 :], axis=0)
    grad_all = grad_all.reshape(feature_blocks, value_blocks, BLOCK, BLOCK)
    left_part = jnp.einsum(
        "iab,ijbc->ijac", feature_all, grad_all, preferred_element_type=jnp.float32
    ).astype(jnp.bfloat16)
    output = jnp.einsum(
        "ijac,jcd->iajd", left_part, value_inverses, preferred_element_type=jnp.float32
    ).astype(jnp.bfloat16)
    output = output.reshape(half_width, value_width)
    return (input_grad, output[None])


def solution(mesh):
    placed = (
        P("section", "dp", "tensor"),
        P("section", "tensor"),
        P("section", "tensor", None),
        P("section", "dp", None),
        P("dp", "tensor"),
        P("section", "tensor", None),
        P("section", "tensor", None),
    )
    return jax.shard_map(
        on_device,
        mesh=mesh,
        in_specs=placed,
        out_specs=(P("section", "dp", "tensor"), P("section", "tensor", None)),
        check_vma=False,
    )
```

profile of v0, /device:TPU:0, one launch (start us, length us, event | category | flops | bytes accessed | tf_op | source)
XLA Modules:
  0.0 384.0 jit_solution(11449314158731028812)
XLA Ops:
  10.5 4.9 %fusion.108 = (f32[128]{0:T(128)S(1)}, f32[128]{0:T(128)S(1)}, f32[128,2048]{1,0:T(8,128)}) fusion(bf16[1,128,2048]{2,1,0:T(8,128)(2,1)} %param.9, f32[2048]{0:T(1024)} %bitcast.105, bf16[1,2048,1024]{2,1,0:T(8,128)(2,1)} %param.11, bf16[1,128,1024]{2,1,0:T(8,128)(2,1)} %param.12), kind=kOutput, calls=%fused_computation.90 | convolution fusion | flops 538443520 | bytes 6038528 | tf_op jit(solution)/shard_map/dot_general | solution.py:62
  15.4 5.9 %all-reduce = (f32[128]{0:T(128)S(1)}, f32[128]{0:T(128)S(1)}) all-reduce(f32[128]{0:T(128)S(1)} %get-tuple-element.140, f32[128]{0:T(128)S(1)} %get-tuple-element.139), channel_id=1, replica_groups=mesh['section'=4,'dp'=4,'tensor'=2] {'tensor'}, use_global_device_ids=true, to_apply=%region_3.0 | all-reduce | flops 256 | bytes 2048 | tf_op jit(solution)/shard_map/psum | solution.py:68
  25.8 3.2 pad_maximum_fusion
  29.0 7.7 %gather_fusion = bf16[16,512,512]{2,1,0:T(8,128)(2,1)} fusion(bf16[13,512,512]{2,1,0:T(8,128)(2,1)} %pad_maximum_fusion, s32[1024]{0:T(1024)S(1)} %pad_clamp_fusion.2), kind=kCustom, calls=%fused_computation | custom fusion | bytes 16777280 | tf_op jit(solution)/shard_map/jit(_take)/gather | solution.py:98
  36.7 9.5 %select_convert_fusion = bf16[16,512,512]{2,1,0:T(8,128)(2,1)} fusion(bf16[16,512,512]{2,1,0:T(8,128)(2,1)} %gather_fusion, pred[16]{0:T(512)(128)(4,1)S(1)} %get-tuple-element.154, pred[16]{0:T(512)(128)(4,1)S(1)} %get-tuple-element.153), kind=kLoop, calls=%fused_computation.4 | loop fusion | flops 8388608 | bytes 16777248 | tf_op jit(solution)/shard_map/convert_element_type | solution.py:101
  51.1 68.4 %reduce-scatter.2.cloned.1.call-done = bf16[4,512,512]{2,1,0:T(8,128)(2,1)} async-done(((bf16[16,512,512]{2,1,0:T(8,128)(2,1)}), bf16[4,512,512]{2,1,0:T(8,128)(2,1)}) %reduce-scatter.2.cloned.1.call-update) | async-done | bytes 2097168 | tf_op jit(solution)/shard_map/reduce_scatter | solution.py:100
  119.5 2.9 fusion.15
  122.5 8.0 %fusion.12 = f32[4,512,512]{2,1,0:T(8,128)S(1)} fusion(bf16[4,512,512]{2,1,0:T(8,128)(2,1)S(1)} %copy-done, f32[4]{0:T(128)S(1)} %sqrt.7, f32[512,512]{1,0:T(8,128)S(1)} %fusion.116, f32[512,512]{1,0:T(8,128)S(1)} %fusion.117, pred[4]{0:T(512)(128)(4,1)S(1)} %compare_and_fusion.2), kind=kOutput, calls=%fused_computation.15 | convolution fusion | flops 6447693824 | bytes 8388628 | tf_op jit(solution)/shard_map/cij,cjk->cik/dot_general | solution.py:37
  130.5 8.5 %divide_select_fusion = f32[4,512,512]{2,1,0:T(8,128)S(1)} fusion(f32[4,512,512]{2,1,0:T(8,128)S(1)} %fusion.12, f32[512,512]{1,0:T(8,128)S(1)} %fusion.115, f32[4]{0:T(128)S(1)} %sqrt.7, f32[512,512]{1,0:T(8,128)S(1)} %fusion.117, pred[]{:T(512)} %bitcast.13), kind=kOutput, calls=%fused_computation.40 | convolution fusion | flops 6446645248 | bytes 10485777 | tf_op jit(solution)/shard_map/cij,cjk->cik/dot_general | solution.py:38
  139.0 7.7 %fusion.10 = f32[4,512,512]{2,1,0:T(8,128)S(1)} fusion(f32[4,512,512]{2,1,0:T(8,128)S(1)} %divide_select_fusion, bf16[4,512,512]{2,1,0:T(8,128)(2,1)S(1)} %copy-done, f32[512,512]{1,0:T(8,128)S(1)} %fusion.116, f32[512,512]{1,0:T(8,128)S(1)} %fusion.117, pred[4]{0:T(512)(128)(4,1)S(1)} %compare_and_fusion.2), kind=kOutput, calls=%fused_computation.14 | convolution fusion | flops 6446645248 | bytes 12582916 | tf_op jit(solution)/shard_map/cij,cjk->cik/dot_general | solution.py:37
  146.7 8.1 %fusion.45 = f32[4,512,512]{2,1,0:T(8,128)S(1)} fusion(f32[4,512,512]{2,1,0:T(8,128)S(1)} %divide_select_fusion, f32[4,512,512]{2,1,0:T(8,128)S(1)} %fusion.10, f32[512,512]{1,0:T(8,128)S(1)} %fusion.115, pred[]{:T(512)} %bitcast.12), kind=kOutput, calls=%fused_computation.43 | convolution fusion | flops 6444548096 | bytes 13631489 | tf_op jit(solution)/shard_map/cij,cjk->cik/dot_general | solution.py:38
  154.8 7.7 %fusion.8 = f32[4,512,512]{2,1,0:T(8,128)S(1)} fusion(f32[4,512,512]{2,1,0:T(8,128)S(1)} %fusion.45, bf16[4,512,512]{2,1,0:T(8,128)(2,1)S(1)} %copy-done, f32[512,512]{1,0:T(8,128)S(1)} %fusion.116, f32[512,512]{1,0:T(8,128)S(1)} %fusion.117, pred[4]{0:T(512)(128)(4,1)S(1)} %compare_and_fusion.2), kind=kOutput, calls=%fused_computation.13 | convolution fusion | flops 6446645248 | bytes 12582916 | tf_op jit(solution)/shard_map/cij,cjk->cik/dot_general | solution.py:37
  162.5 7.9 %fusion.48 = f32[4,512,512]{2,1,0:T(8,128)S(1)} fusion(f32[4,512,512]{2,1,0:T(8,128)S(1)} %fusion.45, f32[4,512,512]{2,1,0:T(8,128)S(1)} %fusion.8, f32[512,512]{1,0:T(8,128)S(1)} %fusion.115, pred[]{:T(512)} %bitcast.11), kind=kOutput, calls=%fused_computation.44 | convolution fusion | flops 6444548096 | bytes 13631489 | tf_op jit(solution)/shard_map/cij,cjk->cik/dot_general | solution.py:38
  170.4 7.9 %fusion.6 = f32[4,512,512]{2,1,0:T(8,128)S(1)} fusion(f32[4,512,512]{2,1,0:T(8,128)S(1)} %fusion.48, bf16[4,512,512]{2,1,0:T(8,128)(2,1)S(1)} %copy-done, f32[512,512]{1,0:T(8,128)S(1)} %fusion.116, f32[512,512]{1,0:T(8,128)S(1)} %fusion.117, pred[4]{0:T(512)(128)(4,1)S(1)} %compare_and_fusion.2), kind=kOutput, calls=%fused_computation.12 | convolution fusion | flops 6446645248 | bytes 12582916 | tf_op jit(solution)/shard_map/cij,cjk->cik/dot_general | solution.py:37
  178.3 7.7 %fusion.51 = f32[4,512,512]{2,1,0:T(8,128)S(1)} fusion(f32[4,512,512]{2,1,0:T(8,128)S(1)} %fusion.48, f32[4,512,512]{2,1,0:T(8,128)S(1)} %fusion.6, f32[512,512]{1,0:T(8,128)S(1)} %fusion.115, pred[]{:T(512)} %bitcast.10), kind=kOutput, calls=%fused_computation.45 | convolution fusion | flops 6444548096 | bytes 13631489 | tf_op jit(solution)/shard_map/cij,cjk->cik/dot_general | solution.py:38
  186.0 8.1 %fusion.4 = f32[4,512,512]{2,1,0:T(8,128)S(1)} fusion(f32[4,512,512]{2,1,0:T(8,128)S(1)} %fusion.51, bf16[4,512,512]{2,1,0:T(8,128)(2,1)S(1)} %copy-done, f32[512,512]{1,0:T(8,128)S(1)} %fusion.116, f32[512,512]{1,0:T(8,128)S(1)} %fusion.117, pred[4]{0:T(512)(128)(4,1)S(1)} %compare_and_fusion.2), kind=kOutput, calls=%fused_computation.11 | convolution fusion | flops 6446645248 | bytes 12582916 | tf_op jit(solution)/shard_map/cij,cjk->cik/dot_general | solution.py:37
  194.1 7.7 %fusion.54 = f32[4,512,512]{2,1,0:T(8,128)S(1)} fusion(f32[4,512,512]{2,1,0:T(8,128)S(1)} %fusion.51, f32[4,512,512]{2,1,0:T(8,128)S(1)} %fusion.4, f32[512,512]{1,0:T(8,128)S(1)} %fusion.115, pred[]{:T(512)} %bitcast.9), kind=kOutput, calls=%fused_computation.46 | convolution fusion | flops 6444548096 | bytes 13631489 | tf_op jit(solution)/shard_map/cij,cjk->cik/dot_general | solution.py:38
  201.8 7.9 %fusion.2 = f32[4,512,512]{2,1,0:T(8,128)S(1)} fusion(f32[4,512,512]{2,1,0:T(8,128)S(1)} %fusion.54, bf16[4,512,512]{2,1,0:T(8,128)(2,1)S(1)} %copy-done, f32[512,512]{1,0:T(8,128)S(1)} %fusion.116, f32[512,512]{1,0:T(8,128)S(1)} %fusion.117, pred[4]{0:T(512)(128)(4,1)S(1)} %compare_and_fusion.2), kind=kOutput, calls=%fused_computation.10 | convolution fusion | flops 6446645248 | bytes 12582916 | tf_op jit(solution)/shard_map/cij,cjk->cik/dot_general | solution.py:37
  209.7 8.6 %fusion.16 = bf16[4,512,512]{2,1,0:T(8,128)(2,1)} fusion(bf16[4,512,512]{2,1,0:T(8,128)(2,1)S(1)} %copy-done, f32[4,512,512]{2,1,0:T(8,128)S(1)} %fusion.54, f32[4,512,512]{2,1,0:T(8,128)S(1)} %fusion.2, f32[512,512]{1,0:T(8,128)S(1)} %fusion.115, pred[4]{0:T(512)(128)(4,1)S(1)} %compare_and_fusion.2, pred[]{:T(512)} %bitcast.8), kind=kOutput, calls=%fused_computation.18 | convolution fusion | flops 6447693824 | bytes 13631493 | tf_op jit(solution)/shard_map/cij,cjk->cik/dot_general | solution.py:38
  222.5 54.3 %all-gather.5.cloned.1.call-done = bf16[16,512,512]{2,1,0:T(8,128)(2,1)} async-done(((bf16[4,512,512]{2,1,0:T(8,128)(2,1)}), bf16[16,512,512]{2,1,0:T(8,128)(2,1)}) %all-gather.5.cloned.1.call-update) | async-done | bytes 8388624 | tf_op jit(solution)/shard_map/all_gather | solution.py:117
  276.8 1.9 dynamic-slice_select_fusion
  278.7 45.9 %all-gather.9.cloned.1.call-done = bf16[512,2048]{1,0:T(8,128)(2,1)} async-done(((bf16[128,2048]{1,0:T(8,128)(2,1)}), bf16[512,2048]{1,0:T(8,128)(2,1)}) %all-gather.9.cloned.1.call-update) | async-done | bytes 2097168 | tf_op jit(solution)/shard_map/all_gather | solution.py:15
  324.6 6.7 %while.17 = (s32[]{:T(128)}, f32[128,2048]{1,0:T(8,128)S(1)}, s32[]{:T(128)}, bf16[4,128,2048]{2,1,0:T(8,128)(2,1)}, s32[]{:T(128)}, /*index=5*/s32[]{:T(128)}, s32[]{:T(128)}, s32[]{:T(128)}) while((s32[]{:T(128)}, f32[128,2048]{1,0:T(8,128)S(1)}, s32[]{:T(128)}, bf16[4,128,2048]{2,1,0:T(8,128)(2,1)}, s32[]{:T(128)}, ...), condition=%wide.region_5.6_spmd.clone, body=%wide.region_4.5_spmd.clone.sunk | while | flops 1048584 | bytes 2621603 | solution.py:24
  324.6 1.7 add_select_fusion.2
  326.4 1.6 add_select_fusion.2
  329.7 1.6 add_select_fusion.2
  332.4 6.3 %gather_fusion.1 = bf16[8,512,512]{2,1,0:T(8,128)(2,1)} fusion(bf16[16,512,512]{2,1,0:T(8,128)(2,1)} %all-gather.5.cloned.1.call-done, s32[1024]{0:T(1024)S(1)} %pad_clamp_fusion.1), kind=kCustom, calls=%fused_computation.1 | custom fusion | bytes 8388640 | tf_op jit(solution)/shard_map/jit(_take)/gather | solution.py:121
  338.7 7.3 %copy.34 = bf16[4,2,512,512]{2,3,0,1:T(8,128)(2,1)} copy(bf16[4,2,512,512]{3,2,1,0:T(8,128)(2,1)} %bitcast.101) | data formatting | bytes 8388608 | tf_op jit(solution)/shard_map/jit(_take)/gather | solution.py:121
  346.0 4.1 %gather_fusion.2 = bf16[4,512,512]{2,1,0:T(8,128)(2,1)S(1)} fusion(bf16[16,512,512]{2,1,0:T(8,128)(2,1)} %all-gather.5.cloned.1.call-done, s32[1024]{0:T(1024)S(1)} %pad_clamp_fusion), kind=kCustom, calls=%fused_computation.2 | custom fusion | bytes 4194320 | tf_op jit(solution)/shard_map/jit(_take)/gather | solution.py:120
  350.1 8.2 %convert_bitcast_fusion = bf16[4,512,2,512]{1,3,0,2:T(8,128)(2,1)} fusion(bf16[4,2,512,512]{2,3,0,1:T(8,128)(2,1)} %copy.34, pred[4,2]{0,1:T(4,128)(4,1)S(1)} %copy.33, bf16[4,512,512]{2,1,0:T(8,128)(2,1)S(1)} %gather_fusion.2, pred[4]{0:T(512)(128)(4,1)S(1)} %compare_and_fusion, bf16[2,512,512]{2,1,0:T(8,128)(2,1)} %all-gather.7.cloned.1.call-done), kind=kOutput, calls=%fused_computation.23 | convolution fusion | flops 4302307328 | bytes 11534348 | tf_op jit(solution)/shard_map/ijac,jcd->iajd/dot_general | solution.py:126
  358.3 11.3 %copy.37 = bf16[4,512,2,512]{3,2,1,0:T(2,128)(2,1)} copy(bf16[4,512,2,512]{1,3,0,2:T(8,128)(2,1)} %convert_bitcast_fusion) | data formatting | bytes 8388608 | tf_op jit(solution)/shard_map/convert_element_type | solution.py:128
  369.5 7.7 %broadcast_in_dim_reshape.3 = bf16[1,2048,1024]{2,1,0:T(8,128)(2,1)} reshape(bf16[4,512,2,512]{3,2,1,0:T(2,128)(2,1)} %copy.37) | data formatting | bytes 8388608 | tf_op jit(solution)/shard_map/broadcast_in_dim;reshape | solution.py:130
  (65 shorter events, 14.2 us)
Async XLA Ops:
  7.2 14.2 %copy-start.1 = (bf16[1,128,2048]{2,1,0:T(8,128)(2,1)S(1)}, bf16[1,128,2048]{2,1,0:T(8,128)(2,1)}, u32[]{:S(2)}) copy-start(bf16[1,128,2048]{2,1,0:T(8,128)(2,1)} %param.9) | copy-start | bytes 1572868
  7.2 14.2 %copy-start.7 = (f32[1,2048]{1,0:T(1,128)S(1)}, f32[1,2048]{1,0:T(1,128)}, u32[]{:S(2)}) copy-start(f32[1,2048]{1,0:T(1,128)} %param.10) | copy-start | bytes 24580
  7.2 112.3 %reduce-scatter.2.cloned.1.call-start = ((), (), s32[]{:S(2)}) async-start(), calls=%async_computation.1 | async-start | bytes 10485760 | tf_op jit(solution)/shard_map/reduce_scatter | solution.py:100
  10.5 11.3 %copy-start.5 = (bf16[1,128,1024]{2,1,0:T(8,128)(2,1)S(1)}, bf16[1,128,1024]{2,1,0:T(8,128)(2,1)}, u32[]{:S(2)}) copy-start(bf16[1,128,1024]{2,1,0:T(8,128)(2,1)} %param.12) | copy-start | bytes 786436
  46.2 0.7 copy-start.8
  46.2 230.6 %all-gather.5.cloned.1.call-start = ((), (), s32[]{:S(2)}) async-start(), calls=%async_computation.2 | async-start | bytes 10485760 | tf_op jit(solution)/shard_map/all_gather | solution.py:117
  119.5 3.0 copy-start
  209.7 8.7 %copy-start.2 = (bf16[1,128,2048]{2,1,0:T(8,128)(2,1)S(1)}, bf16[1,128,2048]{2,1,0:T(8,128)(2,1)}, u32[]{:S(2)}) copy-start(bf16[1,128,2048]{2,1,0:T(8,128)(2,1)} %param.9) | copy-start | bytes 1572868
  209.7 8.7 %copy-start.3 = (f32[128,2048]{1,0:T(8,128)S(1)}, f32[128,2048]{1,0:T(8,128)}, u32[]{:S(2)}) copy-start(f32[128,2048]{1,0:T(8,128)} %get-tuple-element.157) | copy-start | bytes 3145732
  218.3 1.2 copy-start.9
  218.3 106.3 %all-gather.9.cloned.1.call-start = ((), (), s32[]{:S(2)}) async-start(), calls=%async_computation.4 | async-start | bytes 2621440 | tf_op jit(solution)/shard_map/all_gather | solution.py:15
  219.5 130.6 %all-gather.7.cloned.1.call-start = ((), (), s32[]{:S(2)}) async-start(), calls=%async_computation.3 | async-start | bytes 1572864 | tf_op jit(solution)/shard_map/all_gather | solution.py:119
  324.6 6.7 %copy-start.4 = (f32[128,2048]{1,0:T(8,128)S(1)}, f32[128,2048]{1,0:T(8,128)}, u32[]{:S(2)}) copy-start(f32[128,2048]{1,0:T(8,128)} %get-tuple-element.157) | copy-start | bytes 3145732
  324.6 6.7 %copy-start.6 = (bf16[128,2048]{1,0:T(8,128)(2,1)S(1)}, bf16[128,2048]{1,0:T(8,128)(2,1)}, u32[]{:S(2)}) copy-start(bf16[128,2048]{1,0:T(8,128)(2,1)} %param.13) | copy-start | bytes 1572868
Sparse Core Ops, SparseCore 0:
  46.3 73.1 reduce-scatter.1
  218.5 58.2 all-gather.4
  278.9 45.6 all-gather.8
  326.0 20.0 all-gather.6
where the time goes:
time: 391 us; the launch traced here: 384 us
  waiting for transfers between devices  169 us (43%)
  matrix products  112 us (29%)
  local copies, waits for them, and re-layouts  48.8 us (12%)
  other arithmetic  29.1 us (7%)
  between operations  19.5 us (5%)
  blocking collectives  5.87 us (2%)
    reduce_scatter x1, waiting for transfers between devices, on_device(): lax.psum_scatter(packed.astype(jnp.bfloat16), 'dp', scatter_dimension=0,...  68.4 us
    all_gather x1, waiting for transfers between devices, on_device(): gathered = lax.all_gather(owned_blocks, 'dp', axis=0, tiled=True)  54.3 us
    dot_general x6, matrix products, newton_schulz(): jnp.einsum('cij,cjk->cik', approx, 2.0 * identity[None] - product, precis...  48.6 us
    dot_general x6, matrix products, newton_schulz(): jnp.einsum('cij,cjk->cik', matrices, approx, precision=HIGHEST_PREC)  47.1 us
    all_gather x1, waiting for transfers between devices, entering(): everything = lax.all_gather(value.astype(jnp.bfloat16), axis)  45.9 us
    gather x2, local copies, waits for them, and re-layouts, on_device(): grad_all = jnp.take(gathered, slot_table[feature_blocks + 1:], axis=0)  13.6 us
    convert_element_type x1, local copies, waits for them, and re-layouts, on_device(): output = jnp.einsum('ijac,jcd->iajd', left_part, value_inverses, preferre...  11.3 us
    convert_element_type x1, other arithmetic, on_device(): packed.astype(jnp.bfloat16)  9.52 us
  transfers between devices with their start and end apart: 4, of which 3 were waited for; matrix products, arithmetic and copies ran while one was open for 8% of the time, Pallas kernels for 0%

commit v1 on v0

--- a/solution.py
+++ b/solution.py
@@ -114,7 +114,17 @@
     own_limits = jnp.broadcast_to(own_limit, (capacity,))
     inverses = newton_schulz(matrices, own_limits)
     owned_blocks = jnp.where(is_factor[:, None, None], inverses, summed).astype(jnp.bfloat16)
-    gathered = lax.all_gather(owned_blocks, "dp", axis=0, tiled=True)
+    size, mine, span = (lax.axis_size("dp"), lax.axis_index("dp"), owned_blocks.shape[0])
+    forward = [(i, (i + 1) % size) for i in range(size)]
+    gathered = jnp.zeros(
+        (*owned_blocks.shape[:0], size * span, *owned_blocks.shape[0 + 1 :]), owned_blocks.dtype
+    )
+    carried = owned_blocks
+    for step in range(size):
+        owner = (mine - step) % size
+        gathered = lax.dynamic_update_slice_in_dim(gathered, carried, owner * span, axis=0)
+        if step < size - 1:
+            carried = lax.ppermute(carried, "dp", forward)
     value_inverse = jnp.take(gathered, slot_table[feature_blocks], axis=0)
     value_inverses = lax.all_gather(value_inverse[None], "tensor", axis=0, tiled=True)
     feature_all = jnp.take(gathered, slot_table[:feature_blocks], axis=0)

time: 391 us -> 372 us (0.951)
  waiting for transfers between devices: 169 us -> 136 us
  local copies, waits for them, and re-layouts: 48.8 us -> 62 us
    ppermute x0 -> x3, waiting for transfers between devices: none -> 66.6 us  [on_device(): carried = lax.ppermute(carried, 'dp', forward)]
    all_gather x1 -> x0, waiting for transfers between devices: 54.3 us -> none  [on_device(): gathered = lax.all_gather(owned_blocks, 'dp', axis=0, tiled=True)]
    all_gather x1, waiting for transfers between devices: 45.9 us -> 0.03 us  [entering(): everything = lax.all_gather(value.astype(jnp.bfloat16), axis)]
    dynamic_update_slice x0 -> x3, local copies, waits for them, and re-layouts: none -> 9.19 us  [on_device(): lax.dynamic_update_slice_in_dim(gathered, carried, owner * span, axis=0)]
  transfers between devices with their start and end apart: 4 -> 6, of which waited for: 3 -> 4; matrix products, arithmetic and copies ran while one was open for 8% -> 11% of each run, Pallas kernels for 0% -> 0%
where the time goes in v1:
time: 372 us; the launch traced here: 364 us
  waiting for transfers between devices  136 us (37%)
  matrix products  110 us (30%)
  local copies, waits for them, and re-layouts  62 us (17%)
  other arithmetic  29.1 us (8%)
  between operations  21 us (6%)
  blocking collectives  5.87 us (2%)
    reduce_scatter x1, waiting for transfers between devices, on_device(): lax.psum_scatter(packed.astype(jnp.bfloat16), 'dp', scatter_dimension=0,...  68.9 us
    ppermute x3, waiting for transfers between devices, on_device(): carried = lax.ppermute(carried, 'dp', forward)  66.6 us
    dot_general x6, matrix products, newton_schulz(): jnp.einsum('cij,cjk->cik', approx, 2.0 * identity[None] - product, precis...  47.2 us
    dot_general x6, matrix products, newton_schulz(): jnp.einsum('cij,cjk->cik', matrices, approx, precision=HIGHEST_PREC)  47.1 us
    gather x2, local copies, waits for them, and re-layouts, on_device(): grad_all = jnp.take(gathered, slot_table[feature_blocks + 1:], axis=0)  13.6 us
    convert_element_type x1, local copies, waits for them, and re-layouts, on_device(): output = jnp.einsum('ijac,jcd->iajd', left_part, value_inverses, preferre...  11.2 us
    convert_element_type x1, other arithmetic, on_device(): packed.astype(jnp.bfloat16)  9.51 us
    dynamic_update_slice x3, local copies, waits for them, and re-layouts, on_device(): lax.dynamic_update_slice_in_dim(gathered, carried, owner * span, axis=0)  9.19 us
  transfers between devices with their start and end apart: 6, of which 4 were waited for; matrix products, arithmetic and copies ran while one was open for 11% of the time, Pallas kernels for 0%

profile of v1, /device:TPU:0, one launch (start us, length us, event | category | flops | bytes accessed | tf_op | source)
XLA Modules:
  0.0 364.4 jit_solution(439650509957769553)
XLA Ops:
  11.3 4.9 %fusion.108 = (f32[128]{0:T(128)S(1)}, f32[128]{0:T(128)S(1)}, f32[128,2048]{1,0:T(8,128)}) fusion(bf16[1,128,2048]{2,1,0:T(8,128)(2,1)} %param.9, f32[2048]{0:T(1024)} %bitcast.105, bf16[1,2048,1024]{2,1,0:T(8,128)(2,1)} %param.11, bf16[1,128,1024]{2,1,0:T(8,128)(2,1)} %param.12), kind=kOutput, calls=%fused_computation.90 | convolution fusion | flops 538443520 | bytes 6038528 | tf_op jit(solution)/shard_map/dot_general | solution.py:62
  16.3 5.9 %all-reduce = (f32[128]{0:T(128)S(1)}, f32[128]{0:T(128)S(1)}) all-reduce(f32[128]{0:T(128)S(1)} %get-tuple-element.140, f32[128]{0:T(128)S(1)} %get-tuple-element.139), channel_id=1, replica_groups=mesh['section'=4,'dp'=4,'tensor'=2] {'tensor'}, use_global_device_ids=true, to_apply=%region_3.0 | all-reduce | flops 256 | bytes 2048 | tf_op jit(solution)/shard_map/psum | solution.py:68
  26.6 3.3 pad_maximum_fusion
  29.9 7.7 %gather_fusion = bf16[16,512,512]{2,1,0:T(8,128)(2,1)} fusion(bf16[13,512,512]{2,1,0:T(8,128)(2,1)} %pad_maximum_fusion, s32[1024]{0:T(1024)S(1)} %pad_clamp_fusion.2), kind=kCustom, calls=%fused_computation | custom fusion | bytes 16777280 | tf_op jit(solution)/shard_map/jit(_take)/gather | solution.py:98
  37.5 9.5 %select_convert_fusion = bf16[16,512,512]{2,1,0:T(8,128)(2,1)} fusion(bf16[16,512,512]{2,1,0:T(8,128)(2,1)} %gather_fusion, pred[16]{0:T(512)(128)(4,1)S(1)} %get-tuple-element.154, pred[16]{0:T(512)(128)(4,1)S(1)} %get-tuple-element.153), kind=kLoop, calls=%fused_computation.4 | loop fusion | flops 8388608 | bytes 16777248 | tf_op jit(solution)/shard_map/convert_element_type | solution.py:101
  51.5 68.9 %reduce-scatter.2.cloned.1.call-done = bf16[4,512,512]{2,1,0:T(8,128)(2,1)} async-done(((bf16[16,512,512]{2,1,0:T(8,128)(2,1)}), bf16[4,512,512]{2,1,0:T(8,128)(2,1)}) %reduce-scatter.2.cloned.1.call-update) | async-done | bytes 2097168 | tf_op jit(solution)/shard_map/reduce_scatter | solution.py:100
  123.4 8.0 %fusion.12 = f32[4,512,512]{2,1,0:T(8,128)S(1)} fusion(bf16[4,512,512]{2,1,0:T(8,128)(2,1)S(1)} %copy-done, f32[4]{0:T(128)S(1)} %sqrt.7, f32[512,512]{1,0:T(8,128)S(1)} %fusion.116, f32[512,512]{1,0:T(8,128)S(1)} %fusion.117, pred[4]{0:T(512)(128)(4,1)S(1)} %compare_and_fusion.2), kind=kOutput, calls=%fused_computation.15 | convolution fusion | flops 6447693824 | bytes 8388628 | tf_op jit(solution)/shard_map/cij,cjk->cik/dot_general | solution.py:37
  131.3 8.5 %divide_select_fusion = f32[4,512,512]{2,1,0:T(8,128)S(1)} fusion(f32[4,512,512]{2,1,0:T(8,128)S(1)} %fusion.12, f32[512,512]{1,0:T(8,128)S(1)} %fusion.115, f32[4]{0:T(128)S(1)} %sqrt.7, f32[512,512]{1,0:T(8,128)S(1)} %fusion.117, pred[]{:T(512)} %bitcast.13), kind=kOutput, calls=%fused_computation.40 | convolution fusion | flops 6446645248 | bytes 10485777 | tf_op jit(solution)/shard_map/cij,cjk->cik/dot_general | solution.py:38
  139.8 7.7 %fusion.10 = f32[4,512,512]{2,1,0:T(8,128)S(1)} fusion(f32[4,512,512]{2,1,0:T(8,128)S(1)} %divide_select_fusion, bf16[4,512,512]{2,1,0:T(8,128)(2,1)S(1)} %copy-done, f32[512,512]{1,0:T(8,128)S(1)} %fusion.116, f32[512,512]{1,0:T(8,128)S(1)} %fusion.117, pred[4]{0:T(512)(128)(4,1)S(1)} %compare_and_fusion.2), kind=kOutput, calls=%fused_computation.14 | convolution fusion | flops 6446645248 | bytes 12582916 | tf_op jit(solution)/shard_map/cij,cjk->cik/dot_general | solution.py:37
  147.5 8.0 %fusion.45 = f32[4,512,512]{2,1,0:T(8,128)S(1)} fusion(f32[4,512,512]{2,1,0:T(8,128)S(1)} %divide_select_fusion, f32[4,512,512]{2,1,0:T(8,128)S(1)} %fusion.10, f32[512,512]{1,0:T(8,128)S(1)} %fusion.115, pred[]{:T(512)} %bitcast.12), kind=kOutput, calls=%fused_computation.43 | convolution fusion | flops 6444548096 | bytes 13631489 | tf_op jit(solution)/shard_map/cij,cjk->cik/dot_general | solution.py:38
  155.5 7.7 %fusion.8 = f32[4,512,512]{2,1,0:T(8,128)S(1)} fusion(f32[4,512,512]{2,1,0:T(8,128)S(1)} %fusion.45, bf16[4,512,512]{2,1,0:T(8,128)(2,1)S(1)} %copy-done, f32[512,512]{1,0:T(8,128)S(1)} %fusion.116, f32[512,512]{1,0:T(8,128)S(1)} %fusion.117, pred[4]{0:T(512)(128)(4,1)S(1)} %compare_and_fusion.2), kind=kOutput, calls=%fused_computation.13 | convolution fusion | flops 6446645248 | bytes 12582916 | tf_op jit(solution)/shard_map/cij,cjk->cik/dot_general | solution.py:37
  163.1 7.7 %fusion.48 = f32[4,512,512]{2,1,0:T(8,128)S(1)} fusion(f32[4,512,512]{2,1,0:T(8,128)S(1)} %fusion.45, f32[4,512,512]{2,1,0:T(8,128)S(1)} %fusion.8, f32[512,512]{1,0:T(8,128)S(1)} %fusion.115, pred[]{:T(512)} %bitcast.11), kind=kOutput, calls=%fused_computation.44 | convolution fusion | flops 6444548096 | bytes 13631489 | tf_op jit(solution)/shard_map/cij,cjk->cik/dot_general | solution.py:38
  170.9 7.9 %fusion.6 = f32[4,512,512]{2,1,0:T(8,128)S(1)} fusion(f32[4,512,512]{2,1,0:T(8,128)S(1)} %fusion.48, bf16[4,512,512]{2,1,0:T(8,128)(2,1)S(1)} %copy-done, f32[512,512]{1,0:T(8,128)S(1)} %fusion.116, f32[512,512]{1,0:T(8,128)S(1)} %fusion.117, pred[4]{0:T(512)(128)(4,1)S(1)} %compare_and_fusion.2), kind=kOutput, calls=%fused_computation.12 | convolution fusion | flops 6446645248 | bytes 12582916 | tf_op jit(solution)/shard_map/cij,cjk->cik/dot_general | solution.py:37
  178.8 7.6 %fusion.51 = f32[4,512,512]{2,1,0:T(8,128)S(1)} fusion(f32[4,512,512]{2,1,0:T(8,128)S(1)} %fusion.48, f32[4,512,512]{2,1,0:T(8,128)S(1)} %fusion.6, f32[512,512]{1,0:T(8,128)S(1)} %fusion.115, pred[]{:T(512)} %bitcast.10), kind=kOutput, calls=%fused_computation.45 | convolution fusion | flops 6444548096 | bytes 13631489 | tf_op jit(solution)/shard_map/cij,cjk->cik/dot_general | solution.py:38
  186.4 8.1 %fusion.4 = f32[4,512,512]{2,1,0:T(8,128)S(1)} fusion(f32[4,512,512]{2,1,0:T(8,128)S(1)} %fusion.51, bf16[4,512,512]{2,1,0:T(8,128)(2,1)S(1)} %copy-done, f32[512,512]{1,0:T(8,128)S(1)} %fusion.116, f32[512,512]{1,0:T(8,128)S(1)} %fusion.117, pred[4]{0:T(512)(128)(4,1)S(1)} %compare_and_fusion.2), kind=kOutput, calls=%fused_computation.11 | convolution fusion | flops 6446645248 | bytes 12582916 | tf_op jit(solution)/shard_map/cij,cjk->cik/dot_general | solution.py:37
  194.5 7.8 %fusion.54 = f32[4,512,512]{2,1,0:T(8,128)S(1)} fusion(f32[4,512,512]{2,1,0:T(8,128)S(1)} %fusion.51, f32[4,512,512]{2,1,0:T(8,128)S(1)} %fusion.4, f32[512,512]{1,0:T(8,128)S(1)} %fusion.115, pred[]{:T(512)} %bitcast.9), kind=kOutput, calls=%fused_computation.46 | convolution fusion | flops 6444548096 | bytes 13631489 | tf_op jit(solution)/shard_map/cij,cjk->cik/dot_general | solution.py:38
  202.3 7.8 %fusion.2 = f32[4,512,512]{2,1,0:T(8,128)S(1)} fusion(f32[4,512,512]{2,1,0:T(8,128)S(1)} %fusion.54, bf16[4,512,512]{2,1,0:T(8,128)(2,1)S(1)} %copy-done, f32[512,512]{1,0:T(8,128)S(1)} %fusion.116, f32[512,512]{1,0:T(8,128)S(1)} %fusion.117, pred[4]{0:T(512)(128)(4,1)S(1)} %compare_and_fusion.2), kind=kOutput, calls=%fused_computation.10 | convolution fusion | flops 6446645248 | bytes 12582916 | tf_op jit(solution)/shard_map/cij,cjk->cik/dot_general | solution.py:37
  211.0 7.6 %constant_dynamic-update-slice_fusion.3 = (bf16[16,512,512]{2,1,0:T(8,128)(2,1)S(1)}, bf16[4,512,512]{2,1,0:T(8,128)(2,1)S(1)}) fusion(bf16[16,512,512]{2,1,0:T(8,128)(2,1)S(1)} %broadcast_in_dim.160, s32[]{:T(128)S(6)} %select_n.189, bf16[4,512,512]{2,1,0:T(8,128)(2,1)S(1)} %copy-done, f32[4,512,512]{2,1,0:T(8,128)S(1)} %fusion.54, ...), kind=kOutput, calls=%fused_computation.130 | convolution fusion | flops 6447693824 | bytes 19923460 | tf_op jit(solution)/shard_map/cij,cjk->cik/dot_general | solution.py:38
  218.6 3.2 copy-done.1
  221.8 25.6 %collective-permute-done = bf16[4,512,512]{2,1,0:T(8,128)(2,1)} collective-permute-done((bf16[4,512,512]{2,1,0:T(8,128)(2,1)S(1)}, bf16[4,512,512]{2,1,0:T(8,128)(2,1)}, u32[]{:S(2)}, u32[]{:S(2)}) %collective-permute-start) | collective-permute-done | bytes 2097184 | tf_op jit(solution)/shard_map/ppermute | solution.py:127
  248.5 24.7 %collective-permute-done.1 = bf16[4,512,512]{2,1,0:T(8,128)(2,1)} collective-permute-done((bf16[4,512,512]{2,1,0:T(8,128)(2,1)}, bf16[4,512,512]{2,1,0:T(8,128)(2,1)}, u32[]{:S(2)}, u32[]{:S(2)}) %collective-permute-start.1) | collective-permute-done | bytes 2097184 | tf_op jit(solution)/shard_map/ppermute | solution.py:127
  276.6 3.1 constant_dynamic-update-slice_fusion.2
  279.7 3.1 constant_dynamic-update-slice_fusion.1
  282.8 16.4 %collective-permute-done.2 = bf16[4,512,512]{2,1,0:T(8,128)(2,1)} collective-permute-done((bf16[4,512,512]{2,1,0:T(8,128)(2,1)}, bf16[4,512,512]{2,1,0:T(8,128)(2,1)}, u32[]{:S(2)}, u32[]{:S(2)}) %collective-permute-start.2) | collective-permute-done | bytes 2097184 | tf_op jit(solution)/shard_map/ppermute | solution.py:127
  299.1 3.0 constant_dynamic-update-slice_fusion
  304.1 6.7 %while.17 = (s32[]{:T(128)}, f32[128,2048]{1,0:T(8,128)S(1)}, s32[]{:T(128)}, bf16[4,128,2048]{2,1,0:T(8,128)(2,1)}, s32[]{:T(128)}, /*index=5*/s32[]{:T(128)}, s32[]{:T(128)}, s32[]{:T(128)}) while((s32[]{:T(128)}, f32[128,2048]{1,0:T(8,128)S(1)}, s32[]{:T(128)}, bf16[4,128,2048]{2,1,0:T(8,128)(2,1)}, s32[]{:T(128)}, ...), condition=%wide.region_5.6_spmd.clone, body=%wide.region_4.5_spmd.clone.sunk | while | flops 1048584 | bytes 2621603 | solution.py:24
  311.9 6.3 %gather_fusion.1 = bf16[8,512,512]{2,1,0:T(8,128)(2,1)} fusion(bf16[16,512,512]{2,1,0:T(8,128)(2,1)} %constant_dynamic-update-slice_fusion, s32[1024]{0:T(1024)S(1)} %pad_clamp_fusion.1), kind=kCustom, calls=%fused_computation.1 | custom fusion | bytes 8388640 | tf_op jit(solution)/shard_map/jit(_take)/gather | solution.py:131
  318.2 7.3 %copy.40 = bf16[4,2,512,512]{2,3,0,1:T(8,128)(2,1)} copy(bf16[4,2,512,512]{3,2,1,0:T(8,128)(2,1)} %bitcast.101) | data formatting | bytes 8388608 | tf_op jit(solution)/shard_map/jit(_take)/gather | solution.py:131
  325.5 4.1 %gather_fusion.2 = bf16[4,512,512]{2,1,0:T(8,128)(2,1)S(1)} fusion(bf16[16,512,512]{2,1,0:T(8,128)(2,1)} %constant_dynamic-update-slice_fusion, s32[1024]{0:T(1024)S(1)} %pad_clamp_fusion), kind=kCustom, calls=%fused_computation.2 | custom fusion | bytes 4194320 | tf_op jit(solution)/shard_map/jit(_take)/gather | solution.py:130
  329.6 8.2 %convert_bitcast_fusion = bf16[4,512,2,512]{1,3,0,2:T(8,128)(2,1)} fusion(bf16[4,2,512,512]{2,3,0,1:T(8,128)(2,1)} %copy.40, pred[4,2]{0,1:T(4,128)(4,1)S(1)} %copy.39, bf16[4,512,512]{2,1,0:T(8,128)(2,1)S(1)} %gather_fusion.2, pred[4]{0:T(512)(128)(4,1)S(1)} %compare_and_fusion, bf16[2,512,512]{2,1,0:T(8,128)(2,1)} %all-gather.4.cloned.1.call-done), kind=kOutput, calls=%fused_computation.23 | convolution fusion | flops 4302307328 | bytes 11534348 | tf_op jit(solution)/shard_map/ijac,jcd->iajd/dot_general | solution.py:136
  337.8 11.2 %copy.43 = bf16[4,512,2,512]{3,2,1,0:T(2,128)(2,1)} copy(bf16[4,512,2,512]{1,3,0,2:T(8,128)(2,1)} %convert_bitcast_fusion) | data formatting | bytes 8388608 | tf_op jit(solution)/shard_map/convert_element_type | solution.py:138
  349.0 7.7 %broadcast_in_dim_reshape.3 = bf16[1,2048,1024]{2,1,0:T(8,128)(2,1)} reshape(bf16[4,512,2,512]{3,2,1,0:T(2,128)(2,1)} %copy.43) | data formatting | bytes 8388608 | tf_op jit(solution)/shard_map/broadcast_in_dim;reshape | solution.py:140
  (72 shorter events, 25.0 us)
Async XLA Ops:
  8.0 14.2 %copy-start.2 = (bf16[1,128,2048]{2,1,0:T(8,128)(2,1)S(1)}, bf16[1,128,2048]{2,1,0:T(8,128)(2,1)}, u32[]{:S(2)}) copy-start(bf16[1,128,2048]{2,1,0:T(8,128)(2,1)} %param.9) | copy-start | bytes 1572868
  8.0 14.1 %copy-start.7 = (f32[1,2048]{1,0:T(1,128)S(1)}, f32[1,2048]{1,0:T(1,128)}, u32[]{:S(2)}) copy-start(f32[1,2048]{1,0:T(1,128)} %param.10) | copy-start | bytes 24580
  8.0 112.4 %reduce-scatter.2.cloned.1.call-start = ((), (), s32[]{:S(2)}) async-start(), calls=%async_computation.1 | async-start | bytes 10485760 | tf_op jit(solution)/shard_map/reduce_scatter | solution.py:100
  11.3 11.3 %copy-start.5 = (bf16[1,128,1024]{2,1,0:T(8,128)(2,1)S(1)}, bf16[1,128,1024]{2,1,0:T(8,128)(2,1)}, u32[]{:S(2)}) copy-start(bf16[1,128,1024]{2,1,0:T(8,128)(2,1)} %param.12) | copy-start | bytes 786436
  47.1 0.7 copy-start.8
  47.1 257.0 %all-gather.6.cloned.1.call-start = ((), (), s32[]{:S(2)}) async-start(), calls=%async_computation.3 | async-start | bytes 2621440 | tf_op jit(solution)/shard_map/all_gather | solution.py:15
  120.4 3.0 copy-start
  210.9 36.5 %copy-start.3 = (bf16[1,128,2048]{2,1,0:T(8,128)(2,1)S(1)}, bf16[1,128,2048]{2,1,0:T(8,128)(2,1)}, u32[]{:S(2)}) copy-start(bf16[1,128,2048]{2,1,0:T(8,128)(2,1)} %param.9) | copy-start | bytes 1572868
  210.9 36.5 %copy-start.4 = (f32[128,2048]{1,0:T(8,128)S(1)}, f32[128,2048]{1,0:T(8,128)}, u32[]{:S(2)}) copy-start(f32[128,2048]{1,0:T(8,128)} %get-tuple-element.157) | copy-start | bytes 3145732
  210.9 62.5 %copy-start.9 = (s32[1,1,13]{2,1,0:T(1,128)S(1)}, s32[1,1,13]{2,1,0:T(1,128)}, u32[]{:S(2)}) copy-start(s32[1,1,13]{2,1,0:T(1,128)} %param.14) | copy-start | bytes 160
  218.6 3.2 copy-start.1
  221.8 25.6 %collective-permute-start = (bf16[4,512,512]{2,1,0:T(8,128)(2,1)S(1)}, bf16[4,512,512]{2,1,0:T(8,128)(2,1)}, u32[]{:S(2)}, u32[]{:S(2)}) collective-permute-start(bf16[4,512,512]{2,1,0:T(8,128)(2,1)S(1)} %get-tuple-element.161), channel_id=1, source_target_pairs={{0,2},{2,4},{4,6},{6,0},{1,3},{3,5},{5,7},{7,1},{8,10},{10,12},{12... | collective-permute-start | bytes 6291464 | tf_op jit(solution)/shard_map/ppermute | solution.py:127
  247.4 25.8 %collective-permute-start.1 = (bf16[4,512,512]{2,1,0:T(8,128)(2,1)}, bf16[4,512,512]{2,1,0:T(8,128)(2,1)}, u32[]{:S(2)}, u32[]{:S(2)}) collective-permute-start(bf16[4,512,512]{2,1,0:T(8,128)(2,1)} %collective-permute-done), channel_id=1, source_target_pairs={{0,2},{2,4},{4,6},{6,0},{1,3},{3,5},{5,7},{7,1},{8,10},{10,12},{12... | collective-permute-start | bytes 6291464 | tf_op jit(solution)/shard_map/ppermute | solution.py:127
  248.4 81.1 %all-gather.4.cloned.1.call-start = ((), (), s32[]{:S(2)}) async-start(), calls=%async_computation.2 | async-start | bytes 1572864 | tf_op jit(solution)/shard_map/all_gather | solution.py:129
  273.2 26.0 %collective-permute-start.2 = (bf16[4,512,512]{2,1,0:T(8,128)(2,1)}, bf16[4,512,512]{2,1,0:T(8,128)(2,1)}, u32[]{:S(2)}, u32[]{:S(2)}) collective-permute-start(bf16[4,512,512]{2,1,0:T(8,128)(2,1)} %collective-permute-done.1), channel_id=1, source_target_pairs={{0,2},{2,4},{4,6},{6,0},{1,3},{3,5},{5,7},{7,1},{8,10},{10,12},{12... | collective-permute-start | bytes 6291464 | tf_op jit(solution)/shard_map/ppermute | solution.py:127
  304.1 6.7 %copy-start.6 = (bf16[128,2048]{1,0:T(8,128)(2,1)S(1)}, bf16[128,2048]{1,0:T(8,128)(2,1)}, u32[]{:S(2)}) copy-start(bf16[128,2048]{1,0:T(8,128)(2,1)} %param.13) | copy-start | bytes 1572868
Sparse Core Ops, SparseCore 0:
  47.2 73.1 reduce-scatter.1
Sparse Core Ops, SparseCore 1:
  248.5 46.6 all-gather.5
  304.2 21.2 all-gather.3
